TPU v7x, 32 devices: a whole 2x2x4 slice. The times are simulated.
32 devices in a mesh: rep: 4 (over y, x), fsdp: 8 (over z, core).
Axes of the slice: x: 2, y: 2, z: 4, core: 2. Of those that a mesh axis runs over, the one named last changes fastest.
Arguments:
- tokens: bfloat16 [6144, 4096], P(('rep', 'fsdp')), may hold values from -6 to 6
- cotangent: bfloat16 [6144, 256], P(('rep', 'fsdp')), may hold values from -6 to 6
- weight: float32 [4096, 256], P('fsdp'), may hold values from -0.09375 to 0.09375
- momentum: float32 [4, 4096, 256], P('rep', 'fsdp'), may hold values from -6 to 6
- column_order: int32 [64], replicated, may hold values from 0 to 63, each once
Outputs:
- input_grad: bfloat16 [6144, 4096], P(('rep', 'fsdp'))
- new_momentum: float32 [4, 4096, 256], P('rep', 'fsdp')
- update: float32 [4096, 256], P('fsdp')
- new_weight: float32 [4096, 256], P('fsdp')
Inputs may be any that keep to these rules, and one draw needn't show every extreme that they name: `column_order`: each of the 64 frequency indices appears exactly once.
All inputs are finite; a program needn't handle non-finite values.
Results may differ from a plain program's by a relative error of at most 0.0049.
Values may be sent and summed in bfloat16 or wider, within the bound.
No kernel may reach another device: no remote copies, remote signals or barrier semaphores. Data moves between devices by JAX's collectives and lax.ppermute only.
A program may use at most 64 MiB of HBM per device.

v0:
```python
import math
import jax
import jax.numpy as jnp
from jax import lax
from jax.sharding import PartitionSpec as P

KW = 256
BLOCK = 64
SEL = 16
MOMENTUM_DECAY = 0.9
LEARN_RATE = 0.05


def dct_table():
    index = jnp.arange(BLOCK).astype(jnp.float32)
    table = jnp.cos(
        math.pi * (2.0 * index[None, :] + 1.0) * index[:, None] / (2.0 * BLOCK)
    ) * math.sqrt(2.0 / BLOCK)
    return jnp.where(index[:, None] == 0.0, table * math.sqrt(0.5), table)


def on_device(tokens, cotangent, weight, momentum, column_order):
    members = lax.axis_size("fsdp")
    replicas = lax.axis_size("rep")
    rows_own = weight.shape[0]
    table = dct_table()
    weight_half = weight.astype(jnp.bfloat16)
    input_grad = lax.dot_general(
        cotangent,
        lax.all_gather(weight_half, "fsdp", axis=0, tiled=True),
        (((1,), (1,)), ((), ())),
        preferred_element_type=jnp.float32,
    ).astype(jnp.bfloat16)
    scale = float(tokens.shape[0] * members) ** (-0.5)
    weight_grad = (
        lax.psum_scatter(
            lax.dot_general(
                tokens, cotangent, (((0,), (0,)), ((), ())), preferred_element_type=jnp.float32
            ),
            "fsdp",
            scatter_dimension=0,
            tiled=True,
        )
        * scale
    )
    moment = MOMENTUM_DECAY * momentum[0] + weight_grad
    blocks = moment.reshape(rows_own // BLOCK, BLOCK, KW // BLOCK, BLOCK)
    coeffs = jnp.einsum("kn,anbm,lm->akbl", table, blocks, table, precision=lax.Precision.HIGHEST)
    picker = (jnp.arange(BLOCK)[:, None] == column_order[None, :SEL]).astype(jnp.float32)
    compact = jnp.einsum("akbl,ls->akbs", coeffs, picker, precision=lax.Precision.HIGHEST)
    sent = jnp.einsum("akbs,ls->akbl", compact, picker, precision=lax.Precision.HIGHEST)
    own_back = jnp.einsum("kn,akbl,lm->anbm", table, sent, table, precision=lax.Precision.HIGHEST)
    new_momentum = (moment - own_back.reshape(rows_own, KW))[None]
    flat_sent = compact.reshape(-1)
    gathered = lax.all_gather(flat_sent, "rep", axis=0, tiled=True)
    summed = jnp.sum(gathered.reshape(replicas, -1), axis=0)
    summed_full = jnp.einsum(
        "akbs,ls->akbl", summed.reshape(compact.shape), picker, precision=lax.Precision.HIGHEST
    )
    decoded = jnp.einsum(
        "kn,akbl,lm->anbm", table, summed_full, table, precision=lax.Precision.HIGHEST
    )
    update = decoded.reshape(rows_own, KW) / replicas
    new_weight = weight - LEARN_RATE * update
    return (input_grad, new_momentum, update, new_weight)


def solution(mesh):
    in_specs = (
        P(("rep", "fsdp"), None),
        P(("rep", "fsdp"), None),
        P("fsdp", None),
        P("rep", "fsdp", None),
        P(),
    )
    out_specs = (P(("rep", "fsdp"), None), P("rep", "fsdp", None), P("fsdp", None), P("fsdp", None))
    return jax.shard_map(
        on_device, mesh=mesh, in_specs=in_specs, out_specs=out_specs, check_vma=False
    )
```

profile of v0, /device:TPU:0, one launch (start us, length us, event | category | flops | bytes accessed | tf_op | source)
XLA Modules:
  0.0 147.0 jit_solution(15613769380523077113)
XLA Ops:
  7.2 1.9 %convert_element_type.31 = bf16[512,256]{1,0:T(8,128)(2,1)} convert(f32[512,256]{1,0:T(8,128)} %param.7) | non-fusion elementwise | flops 131072 | bytes 786432 | tf_op jit(solution)/shard_map/convert_element_type | solution.py:27
  9.2 3.6 %fusion.78 = f32[4096,256]{1,0:T(8,128)} fusion(bf16[192,4096]{1,0:T(8,128)(2,1)S(1)} %copy-done, bf16[192,256]{1,0:T(8,128)(2,1)} %param.6), kind=kOutput, calls=%fused_computation.85 | convolution fusion | flops 402653184 | bytes 5865472 | tf_op jit(solution)/shard_map/dot_general | solution.py:37
  12.8 1.0 copy-done.2
  14.9 27.2 %all-gather.2.cloned.1.call-done = bf16[4096,256]{1,0:T(8,128)(2,1)} async-done(((bf16[512,256]{1,0:T(8,128)(2,1)}), bf16[4096,256]{1,0:T(8,128)(2,1)}) %all-gather.2.cloned.1.call-update) | async-done | bytes 2097168 | tf_op jit(solution)/shard_map/all_gather | solution.py:30
  42.1 3.6 %convolution_convert_fusion = bf16[192,4096]{1,0:T(8,128)(2,1)} fusion(bf16[192,256]{1,0:T(8,128)(2,1)S(1)} %copy-done.4, bf16[4096,256]{1,0:T(8,128)(2,1)} %all-gather.2.cloned.1.call-done), kind=kOutput, calls=%fused_computation | convolution fusion | flops 403439616 | bytes 3768320 | tf_op jit(solution)/shard_map/dot_general | solution.py:28
  45.6 48.1 %reduce-scatter.2.cloned.1.call-done = f32[512,256]{1,0:T(8,128)} async-done(((f32[4096,256]{1,0:T(8,128)}), f32[512,256]{1,0:T(8,128)}) %reduce-scatter.2.cloned.1.call-update) | async-done | bytes 524304 | tf_op jit(solution)/shard_map/reduce_scatter | solution.py:36
  93.7 1.1 bitcast_add_fusion
  95.3 1.3 fusion.2
  96.6 1.1 convolution_bitcast_fusion.1
  97.8 1.3 fusion.53
  99.5 1.7 %fusion.51 = f32[8,64,4,64]{1,3,2,0:T(8,128)} fusion(f32[8,64,4,16]{1,3,2,0:T(8,128)S(1)} %fusion.53, s32[16]{0:T(128)S(1)} %bitcast.53), kind=kOutput, calls=%fused_computation.59 | convolution fusion | flops 25166848 | bytes 655424 | tf_op jit(solution)/shard_map/akbs,ls->akbl/dot_general | solution.py:51
  101.8 10.9 %all_gather.7 = f32[131072]{0:T(1024)S(1)} all-gather(f32[32768]{0:T(1024)S(1)} %reshape.51), channel_id=1, replica_groups=mesh['rep'=4,'fsdp'=8] {'rep'}, dimensions={0}, use_global_device_ids=true | all-gather | bytes 655360 | tf_op jit(solution)/shard_map/all_gather | solution.py:55
  114.0 1.7 %fusion = f32[8,64,4,64]{1,3,2,0:T(8,128)S(1)} fusion(f32[8,64,4,16]{3,2,1,0:T(4,128)S(1)} %reshape.53, s32[16]{0:T(128)S(1)} %bitcast.54), kind=kOutput, calls=%fused_computation.3 | convolution fusion | flops 25166848 | bytes 655424 | tf_op jit(solution)/shard_map/akbs,ls->akbl/dot_general | solution.py:57
  115.7 3.3 %fusion.6 = f32[8,4,64,64]{2,3,1,0:T(8,128)S(1)} fusion(f32[8,64,4,64]{1,3,2,0:T(8,128)S(1)} %fusion, f32[64]{0:T(128)S(1)} %iota_convert_fusion, f32[64]{0:T(128)S(1)} %add_multiply_fusion, pred[64]{0:T(512)(128)(4,1)S(1)} %broadcast_compare_fusion), kind=kOutput, calls=%fused_computation.13 | convolution fusion | flops 100683776 | bytes 1049152 | tf_op jit(solution)/shard_map/kn,akbl,lm->anbm/dot_general | solution.py:60
  119.0 2.2 %multiply_bitcast_fusion = (f32[8,64,4,64]{3,1,2,0:T(8,128)S(1)}, f32[8,64,4,64]{3,1,2,0:T(8,128)}) fusion(f32[8,4,64,64]{2,3,1,0:T(8,128)S(1)} %fusion.6, f32[64]{0:T(128)S(1)} %iota_convert_fusion, f32[64]{0:T(128)S(1)} %add_multiply_fusion, pred[64]{0:T(512)(128)(4,1)S(1)} %broadcast_compare_fusion), kind=kOutput, calls=%fused_computation.7 | convolution fusion | flops 100945920 | bytes 1573440 | tf_op jit(solution)/shard_map/kn,akbl,lm->anbm/dot_general | solution.py:60
  121.2 1.3 copy.41
  122.5 1.5 %mul.163 = f32[512,256]{0,1:T(8,128)S(1)} reshape(f32[8,64,4,64]{1,0,3,2:T(8,128)} %copy.41) | data formatting | bytes 1048576 | tf_op jit(solution)/shard_map/mul | solution.py:64
  124.0 1.1 sub.7
  126.1 3.0 %copy.52 = f32[8,64,4,64]{3,2,1,0:T(4,128)} copy(f32[8,64,4,64]{3,1,2,0:T(8,128)} %get-tuple-element.17) | data formatting | bytes 1048576
  129.1 2.6 %reshape.56 = f32[512,256]{1,0:T(8,128)} reshape(f32[8,64,4,64]{3,2,1,0:T(4,128)} %copy.52) | data formatting | bytes 1048576
  131.7 3.3 %fusion.9 = f32[8,4,64,64]{2,3,1,0:T(8,128)S(1)} fusion(f32[8,64,4,64]{1,3,2,0:T(8,128)S(1)} %copy-done.1, f32[64]{0:T(128)S(1)} %iota_convert_fusion, f32[64]{0:T(128)S(1)} %add_multiply_fusion, pred[64]{0:T(512)(128)(4,1)S(1)} %broadcast_compare_fusion), kind=kOutput, calls=%fused_computation.16 | convolution fusion | flops 100683776 | bytes 1049152 | tf_op jit(solution)/shard_map/kn,akbl,lm->anbm/dot_general | solution.py:52
  135.0 1.1 convolution_bitcast_fusion
  136.9 1.4 reshape.50
  138.3 1.9 %subtract_bitcast_fusion = f32[1,512,256]{2,1,0:T(8,128)} fusion(f32[512,256]{1,0:T(8,128)S(1)} %bitcast_add_fusion, f32[512,256]{1,0:T(8,128)} %reshape.50), kind=kLoop, calls=%fused_computation.10 | loop fusion | flops 131072 | bytes 1572864 | tf_op jit(solution)/shard_map/broadcast_in_dim | solution.py:53
  (27 shorter events, 5.6 us)
Async XLA Ops:
  7.2 2.0 %copy-start = (bf16[192,4096]{1,0:T(8,128)(2,1)S(1)}, bf16[192,4096]{1,0:T(8,128)(2,1)}, u32[]{:S(2)}) copy-start(bf16[192,4096]{1,0:T(8,128)(2,1)} %param.5) | copy-start | bytes 4718596
  7.2 34.9 %all-gather.2.cloned.1.call-start = ((), (), s32[]{:S(2)}) async-start(), calls=%async_computation.1 | async-start | bytes 2359296 | tf_op jit(solution)/shard_map/all_gather | solution.py:30
  9.1 84.6 %reduce-scatter.2.cloned.1.call-start = ((), (), s32[]{:S(2)}) async-start(), calls=%async_computation.2 | async-start | bytes 4718592 | tf_op jit(solution)/shard_map/reduce_scatter | solution.py:36
  12.8 1.0 copy-start.2
  12.8 29.3 %copy-start.4 = (bf16[192,256]{1,0:T(8,128)(2,1)S(1)}, bf16[192,256]{1,0:T(8,128)(2,1)}, u32[]{:S(2)}) copy-start(bf16[192,256]{1,0:T(8,128)(2,1)} %param.6) | copy-start | bytes 294916
  14.8 78.9 %copy-start.3 = (f32[1,512,256]{2,1,0:T(8,128)S(1)}, f32[1,512,256]{2,1,0:T(8,128)}, u32[]{:S(2)}) copy-start(f32[1,512,256]{2,1,0:T(8,128)} %param.8) | copy-start | bytes 1572868
  95.3 2.5 %copy-start.5 = (s32[64]{0:T(128)S(1)}, s32[64]{0:T(128)}, u32[]{:S(2)}) copy-start(s32[64]{0:T(128)} %param.9) | copy-start | bytes 772
  126.1 5.6 %copy-start.1 = (f32[8,64,4,64]{1,3,2,0:T(8,128)S(1)}, f32[8,64,4,64]{1,3,2,0:T(8,128)}, u32[]{:S(2)}) copy-start(f32[8,64,4,64]{1,3,2,0:T(8,128)} %fusion.51) | copy-start | bytes 1572868
Sparse Core Ops, SparseCore 0:
  10.2 31.8 all-gather.1
  44.4 49.3 reduce-scatter.1
where the time goes:
time: 147 us
  waiting for transfers between devices  75.3 us (51%)
  matrix products  24.2 us (16%)
  local copies, waits for them, and re-layouts  16 us (11%)
  between operations  14.2 us (10%)
  blocking collectives  10.9 us (7%)
  other arithmetic  6.36 us (4%)
    reduce_scatter x1, waiting for transfers between devices, on_device(): lax.psum_scatter(lax.dot_general(tokens, cotangent, (((0,), (0,)), ((), (...  48.1 us
    all_gather x1, waiting for transfers between devices, on_device(): lax.all_gather(weight_half, 'fsdp', axis=0, tiled=True)  27.2 us
    all_gather x1, blocking collectives, on_device(): gathered = lax.all_gather(flat_sent, 'rep', axis=0, tiled=True)  10.9 us
    unnamed x16, local copies, waits for them, and re-layouts  8.64 us
    dot_general x2, matrix products, on_device(): jnp.einsum('kn,akbl,lm->anbm', table, summed_full, table, precision=lax.P...  5.46 us
    dot_general x2, matrix products, on_device(): jnp.einsum('kn,akbl,lm->anbm', table, sent, table, precision=lax.Precisio...  4.42 us
    dot_general x1, matrix products, on_device(): lax.dot_general(tokens, cotangent, (((0,), (0,)), ((), ())), preferred_el...  3.61 us
    dot_general x1, matrix products, on_device(): lax.dot_general(cotangent, lax.all_gather(weight_half, 'fsdp', axis=0, ti...  3.58 us
  transfers between devices with their start and end apart: 2, of which 2 were waited for; matrix products, arithmetic and copies ran while one was open for 6% of the time, Pallas kernels for 0%

commit v1 on v0

--- a/solution.py
+++ b/solution.py
@@ -9,6 +9,28 @@
 SEL = 16
 MOMENTUM_DECAY = 0.9
 LEARN_RATE = 0.05
+
+
+def laid_out(pieces, dim):
+    dims = list(pieces.shape[1:])
+    dims[dim] *= pieces.shape[0]
+    return jnp.moveaxis(pieces, 0, dim).reshape(dims)
+
+
+def collected_by_bits(x, axis):
+    length = lax.axis_size(axis)
+    tiles = x[None]
+    for level in range(length.bit_length() - 1):
+        stride = 1 << level
+        other = lax.ppermute(tiles, axis, [(i, i ^ stride) for i in range(length)])
+        both = jnp.stack([tiles, other])
+        upper = lax.axis_index(axis) >> level & 1
+        tiles = jnp.where(upper == 0, both, both[::-1]).reshape(-1, *x.shape)
+    return tiles
+
+
+def collect(x, axis, dim):
+    return laid_out(collected_by_bits(x, axis), dim)
 
 
 def dct_table():
@@ -27,7 +49,7 @@
     weight_half = weight.astype(jnp.bfloat16)
     input_grad = lax.dot_general(
         cotangent,
-        lax.all_gather(weight_half, "fsdp", axis=0, tiled=True),
+        collect(weight_half, "fsdp", 0),
         (((1,), (1,)), ((), ())),
         preferred_element_type=jnp.float32,
     ).astype(jnp.bfloat16)

time: 147 us -> 174 us (1.18)
  waiting for transfers between devices: 75.3 us -> 91.2 us
  starting transfers between devices: 0.08 us -> 6.15 us
  local copies, waits for them, and re-layouts: 16 us -> 20.8 us
  other arithmetic: 6.36 us -> 8.83 us
    ppermute x0 -> x3, waiting for transfers between devices: none -> 91.2 us  [collected_by_bits(): other = lax.ppermute(tiles, axis, [(i, i ^ stride) for i in range(length)])]
    reduce_scatter x1, waiting for transfers between devices: 48.1 us -> 0.01 us  [on_device(): lax.psum_scatter(lax.dot_general(tokens, cotangent, (((0,), (0,)), ((), (...]
    all_gather x1 -> x0, waiting for transfers between devices: 27.2 us -> none  [on_device(): lax.all_gather(weight_half, 'fsdp', axis=0, tiled=True)]
    ppermute x0 -> x3, starting transfers between devices: none -> 6.11 us  [collected_by_bits(): other = lax.ppermute(tiles, axis, [(i, i ^ stride) for i in range(length)])]
    another operation x0 -> x5, other arithmetic: none -> 2.77 us  [collected_by_bits(): both = jnp.stack([tiles, other])]
    convert_element_type x1 -> x0, other arithmetic: 1.88 us -> none  [on_device(): weight_half = weight.astype(jnp.bfloat16)]
    unnamed x16 -> x18, local copies, waits for them, and re-layouts: 8.64 us -> 10.2 us
  transfers between devices with their start and end apart: 2 -> 4, of which waited for: 2 -> 3; matrix products, arithmetic and copies ran while one was open for 6% -> 4% of each run, Pallas kernels for 0% -> 0%
where the time goes in v1:
time: 174 us
  waiting for transfers between devices  91.2 us (52%)
  matrix products  22.6 us (13%)
  local copies, waits for them, and re-layouts  20.8 us (12%)
  between operations  14.2 us (8%)
  blocking collectives  10.2 us (6%)
  other arithmetic  8.83 us (5%)
  starting transfers between devices  6.15 us (4%)
    ppermute x3, waiting for transfers between devices, collected_by_bits(): other = lax.ppermute(tiles, axis, [(i, i ^ stride) for i in range(length)])  91.2 us
    all_gather x1, blocking collectives, on_device(): gathered = lax.all_gather(flat_sent, 'rep', axis=0, tiled=True)  10.2 us
    unnamed x18, local copies, waits for them, and re-layouts  10.2 us
    ppermute x3, starting transfers between devices, collected_by_bits(): other = lax.ppermute(tiles, axis, [(i, i ^ stride) for i in range(length)])  6.11 us
    dot_general x2, matrix products, on_device(): jnp.einsum('kn,akbl,lm->anbm', table, summed_full, table, precision=lax.P...  5.41 us
    dot_general x2, matrix products, on_device(): jnp.einsum('kn,akbl,lm->anbm', table, sent, table, precision=lax.Precisio...  4.42 us
    mul x2, local copies, waits for them, and re-layouts, on_device(): new_weight = weight - LEARN_RATE * update  3.7 us
    dot_general x1, matrix products, on_device(): lax.dot_general(tokens, cotangent, (((0,), (0,)), ((), ())), preferred_el...  3.62 us
  transfers between devices with their start and end apart: 4, of which 3 were waited for; matrix products, arithmetic and copies ran while one was open for 4% of the time, Pallas kernels for 0%

profile of v1, /device:TPU:0, one launch (start us, length us, event | category | flops | bytes accessed | tf_op | source)
XLA Modules:
  0.0 173.9 jit_solution(7560440732032471648)
XLA Ops:
  7.2 1.4 copy-done
  8.6 3.6 %fusion.81 = f32[4096,256]{1,0:T(8,128)} fusion(bf16[192,4096]{1,0:T(8,128)(2,1)S(1)} %copy-done, bf16[192,256]{1,0:T(8,128)(2,1)} %param.6), kind=kOutput, calls=%fused_computation.96 | convolution fusion | flops 402653184 | bytes 5865472 | tf_op jit(solution)/shard_map/dot_general | solution.py:59
  15.2 3.0 %collective-permute-start.1 = (bf16[2,512,256]{2,1,0:T(8,128)(2,1)S(1)}, bf16[2,512,256]{2,1,0:T(8,128)(2,1)}, u32[]{:S(2)}, u32[]{:S(2)}) collective-permute-start(bf16[2,512,256]{2,1,0:T(8,128)(2,1)S(1)} %get-tuple-element.19), channel_id=1, source_target_pairs={{0,2},{1,3},{2,0},{3,1},{4,6},{5,7},{6,4},{7,5},{8,10},{9,11},{10,... | collective-permute-start | bytes 1572872 | tf_op jit(solution)/shard_map/ppermute | solution.py:25
  18.2 21.1 %collective-permute-done.1 = bf16[2,512,256]{2,1,0:T(8,128)(2,1)} collective-permute-done((bf16[2,512,256]{2,1,0:T(8,128)(2,1)S(1)}, bf16[2,512,256]{2,1,0:T(8,128)(2,1)}, u32[]{:S(2)}, u32[]{:S(2)}) %collective-permute-start.1) | collective-permute-done | bytes 524320 | tf_op jit(solution)/shard_map/ppermute | solution.py:25
  40.6 2.6 %collective-permute-start.2 = (bf16[4,512,256]{2,1,0:T(8,128)(2,1)S(1)}, bf16[4,512,256]{2,1,0:T(8,128)(2,1)}, u32[]{:S(2)}, u32[]{:S(2)}) collective-permute-start(bf16[4,512,256]{2,1,0:T(8,128)(2,1)S(1)} %bitcast.69), channel_id=1, source_target_pairs={{0,4},{1,5},{2,6},{3,7},{4,0},{5,1},{6,2},{7,3},{8,12},{9,13},{10,... | collective-permute-start | bytes 3145736 | tf_op jit(solution)/shard_map/ppermute | solution.py:25
  44.2 68.9 %collective-permute-done.2 = bf16[4,512,256]{2,1,0:T(8,128)(2,1)} collective-permute-done((bf16[4,512,256]{2,1,0:T(8,128)(2,1)S(1)}, bf16[4,512,256]{2,1,0:T(8,128)(2,1)}, u32[]{:S(2)}, u32[]{:S(2)}) %collective-permute-start.2) | collective-permute-done | bytes 1048608 | tf_op jit(solution)/shard_map/ppermute | solution.py:25
  113.1 1.4 pad_maximum_fusion
  115.4 2.0 %fusion = bf16[192,4096]{1,0:T(8,128)(2,1)} fusion(bf16[4096,256]{1,0:T(8,128)(2,1)S(1)} %bitcast.68, bf16[192,256]{1,0:T(8,128)(2,1)S(1)} %copy-done.5), kind=kOutput, calls=%fused_computation.1 | convolution fusion | flops 403439616 | bytes 3768320 | tf_op jit(solution)/shard_map/dot_general | solution.py:50
  121.5 1.3 fusion.56
  123.2 1.7 fusion.54
  125.6 10.2 %all_gather.3 = f32[131072]{0:T(1024)S(1)} all-gather(f32[32768]{0:T(1024)S(1)} %reshape.59), channel_id=1, replica_groups=mesh['rep'=4,'fsdp'=8] {'rep'}, dimensions={0}, use_global_device_ids=true | all-gather | bytes 655360 | tf_op jit(solution)/shard_map/all_gather | solution.py:77
  137.0 1.7 fusion.1
  138.7 3.3 %fusion.9 = f32[8,4,64,64]{2,3,1,0:T(8,128)S(1)} fusion(f32[8,64,4,64]{1,3,2,0:T(8,128)S(1)} %fusion.1, f32[64]{0:T(128)S(1)} %iota_convert_fusion, f32[64]{0:T(128)S(1)} %add_multiply_fusion, pred[64]{0:T(512)(128)(4,1)S(1)} %broadcast_compare_fusion), kind=kOutput, calls=%fused_computation.24 | convolution fusion | flops 100683776 | bytes 1049152 | tf_op jit(solution)/shard_map/kn,akbl,lm->anbm/dot_general | solution.py:82
  142.0 2.1 %multiply_bitcast_fusion = (f32[8,64,4,64]{3,1,2,0:T(8,128)S(1)}, f32[8,64,4,64]{3,1,2,0:T(8,128)}) fusion(f32[8,4,64,64]{2,3,1,0:T(8,128)S(1)} %fusion.9, f32[64]{0:T(128)S(1)} %iota_convert_fusion, f32[64]{0:T(128)S(1)} %add_multiply_fusion, pred[64]{0:T(512)(128)(4,1)S(1)} %broadcast_compare_fusion), kind=kOutput, calls=%fused_computation.12 | convolution fusion | flops 100945920 | bytes 1573440 | tf_op jit(solution)/shard_map/kn,akbl,lm->anbm/dot_general | solution.py:82
  144.2 1.3 copy.41
  145.5 2.4 %mul.163 = f32[512,256]{0,1:T(8,128)} reshape(f32[8,64,4,64]{1,0,3,2:T(8,128)} %copy.41) | data formatting | bytes 1048576 | tf_op jit(solution)/shard_map/mul | solution.py:86
  147.9 2.1 %sub.7 = f32[512,256]{0,1:T(8,128)} subtract(f32[512,256]{0,1:T(8,128)} %copy.42, f32[512,256]{0,1:T(8,128)} %mul.163) | non-fusion elementwise | flops 131072 | bytes 1572864 | tf_op jit(solution)/shard_map/sub | solution.py:86
  149.9 2.0 %copy.44 = f32[512,256]{1,0:T(8,128)} copy(f32[512,256]{0,1:T(8,128)} %sub.7) | data formatting | bytes 1048576
  152.0 3.3 %fusion.12 = f32[8,4,64,64]{2,3,1,0:T(8,128)S(1)} fusion(f32[8,64,4,64]{1,3,2,0:T(8,128)S(1)} %copy-done.1, f32[64]{0:T(128)S(1)} %iota_convert_fusion, f32[64]{0:T(128)S(1)} %add_multiply_fusion, pred[64]{0:T(512)(128)(4,1)S(1)} %broadcast_compare_fusion), kind=kOutput, calls=%fused_computation.27 | convolution fusion | flops 100683776 | bytes 1049152 | tf_op jit(solution)/shard_map/kn,akbl,lm->anbm/dot_general | solution.py:74
  156.4 1.7 copy.35
  158.1 2.7 %reshape.58 = f32[512,256]{1,0:T(8,128)} reshape(f32[8,64,4,64]{3,2,1,0:T(4,128)} %copy.35) | data formatting | bytes 1048576 | tf_op jit(solution)/shard_map/reshape | solution.py:75
  160.8 1.9 %subtract_bitcast_fusion = f32[1,512,256]{2,1,0:T(8,128)} fusion(f32[512,256]{1,0:T(8,128)S(1)} %bitcast_add_fusion, f32[512,256]{1,0:T(8,128)} %reshape.58), kind=kLoop, calls=%fused_computation.17 | loop fusion | flops 131072 | bytes 1572864 | tf_op jit(solution)/shard_map/broadcast_in_dim | solution.py:75
  162.7 1.7 copy.52
  164.4 2.6 %reshape.64 = f32[512,256]{1,0:T(8,128)} reshape(f32[8,64,4,64]{3,2,1,0:T(4,128)} %copy.52) | data formatting | bytes 1048576
  (38 shorter events, 13.8 us)
Async XLA Ops:
  7.2 1.4 copy-start
  7.2 110.2 %reduce-scatter.2.cloned.1.call-start = ((), (), s32[]{:S(2)}) async-start(), calls=%async_computation.1 | async-start | bytes 4718592 | tf_op jit(solution)/shard_map/reduce_scatter | solution.py:58
  12.2 1.0 copy-start.3
  13.3 1.7 collective-permute-start
  15.2 24.1 %collective-permute-start.1 = (bf16[2,512,256]{2,1,0:T(8,128)(2,1)S(1)}, bf16[2,512,256]{2,1,0:T(8,128)(2,1)}, u32[]{:S(2)}, u32[]{:S(2)}) collective-permute-start(bf16[2,512,256]{2,1,0:T(8,128)(2,1)S(1)} %get-tuple-element.19), channel_id=1, source_target_pairs={{0,2},{1,3},{2,0},{3,1},{4,6},{5,7},{6,4},{7,5},{8,10},{9,11},{10,... | collective-permute-start | bytes 1572872 | tf_op jit(solution)/shard_map/ppermute | solution.py:25
  40.6 72.5 %collective-permute-start.2 = (bf16[4,512,256]{2,1,0:T(8,128)(2,1)S(1)}, bf16[4,512,256]{2,1,0:T(8,128)(2,1)}, u32[]{:S(2)}, u32[]{:S(2)}) collective-permute-start(bf16[4,512,256]{2,1,0:T(8,128)(2,1)S(1)} %bitcast.69), channel_id=1, source_target_pairs={{0,4},{1,5},{2,6},{3,7},{4,0},{5,1},{6,2},{7,3},{8,12},{9,13},{10,... | collective-permute-start | bytes 3145736 | tf_op jit(solution)/shard_map/ppermute | solution.py:25
  114.5 0.9 copy-start.5
  115.4 2.0 %copy-start.4 = (f32[1,512,256]{2,1,0:T(8,128)S(1)}, f32[1,512,256]{2,1,0:T(8,128)}, u32[]{:S(2)}) copy-start(f32[1,512,256]{2,1,0:T(8,128)} %param.8) | copy-start | bytes 1572868
  119.0 2.5 %copy-start.6 = (s32[64]{0:T(128)S(1)}, s32[64]{0:T(128)}, u32[]{:S(2)}) copy-start(s32[64]{0:T(128)} %param.9) | copy-start | bytes 772
  145.5 6.5 %copy-start.1 = (f32[8,64,4,64]{1,3,2,0:T(8,128)S(1)}, f32[8,64,4,64]{1,3,2,0:T(8,128)}, u32[]{:S(2)}) copy-start(f32[8,64,4,64]{1,3,2,0:T(8,128)} %fusion.54) | copy-start | bytes 1572868
  158.1 4.6 %copy-start.2 = (f32[8,64,4,64]{3,1,2,0:T(8,128)S(1)}, f32[8,64,4,64]{3,1,2,0:T(8,128)}, u32[]{:S(2)}) copy-start(f32[8,64,4,64]{3,1,2,0:T(8,128)} %get-tuple-element.17) | copy-start | bytes 1572868
Sparse Core Ops, SparseCore 0:
  12.3 83.0 reduce-scatter.1
